TPU v7x, 128 devices: a whole 4x4x4 slice. The times are simulated.
128 devices in a mesh: row: 16 (over x, z), col: 4 (over y_hi, core), tm: 2 (over y_lo).
Axes of the slice: x: 4, y: 4 (y_hi: 2, y_lo: 2; y = y_hi * 2 + y_lo), z: 4, core: 2. Of those that a mesh axis runs over, the one named last changes fastest.
Arguments:
- samples: bfloat16 [1024, 16, 2, 4096], P('row', None, 'tm', 'col'), may hold values from -6 to 6
- whitening: bfloat16 [1024, 1024], replicated, may hold values from -0.1875 to 0.1875
- ridge: float32 [2048], P('col'), may hold values from 2 to 20
- slab_start: int32 [1], replicated, may hold values from 0 to 63
- panels: int32 [4], replicated, may hold values from 0 to 3, as said below
Outputs:
- trailing: float32 [131072, 2048], P(('row', 'tm'), 'col')
- factor: bfloat16 [2, 131072, 512], P(None, ('row', 'tm'))
Inputs may be any that keep to these rules, and one draw needn't show every extreme that they name: `panels`: each panel index once.
All inputs are finite; a program needn't handle non-finite values.
Results may differ from a plain program's by a relative error of at most 0.012.
The roundings to bfloat16 on the way count: a program that leaves them out, or rounds other values in their place, can miss the bound.
Values may be sent and summed in bfloat16 or wider, within the bound.
No kernel may reach another device: no remote copies, remote signals or barrier semaphores. Data moves between devices by JAX's collectives and lax.ppermute only.
A program may use at most 192 MiB of HBM per device.

v0:
```python
import jax
import jax.numpy as jnp
from jax import lax
from jax.sharding import PartitionSpec as P

S = 1024
PANEL = 512
PANELS = 2


def broadcast(block, axis, holder):
    block = jnp.where(lax.axis_index(axis) == holder, block, jnp.zeros_like(block))
    return lax.psum(block, axis)


def rows_for(lines, devices):
    spare = -lines.shape[0] % devices
    if not spare:
        return lines
    return jnp.concatenate([lines, jnp.zeros((spare, *lines.shape[1:]), lines.dtype)])


def from_root(shard, axis, root):
    lines = jnp.where(lax.axis_index(axis) == root, shard, jnp.zeros_like(shard)).reshape(
        -1, *shard.shape[1:][-1:]
    )
    padded = rows_for(lines, lax.axis_size(axis))
    own = lax.psum_scatter(padded, axis, scatter_dimension=0, tiled=True)
    return lax.all_gather(own, axis, axis=0, tiled=True)[: len(lines)].reshape(shard.shape)


def broadcast_2(shard, axis, root):
    return lax.dynamic_index_in_dim(lax.all_gather(shard, axis), root, 0, keepdims=False)


def on_device(samples, whitening, ridge, slab_start, panels):
    moved = lax.all_to_all(samples, "row", split_axis=1, concat_axis=0, tiled=True)
    local_width = moved.shape[3]
    series = moved.reshape(moved.shape[0], local_width)
    whitened = jnp.dot(whitening, series, preferred_element_type=jnp.float32).astype(jnp.bfloat16)
    col_count = lax.axis_size("col")
    tm_count = lax.axis_size("tm")
    rows_here = col_count * local_width
    slab_width = PANEL * col_count
    scale = S ** (-0.5)
    slab_first = slab_start[0] * slab_width
    owner_index = slab_first // rows_here
    slab_offset = slab_first % rows_here
    col_index = lax.axis_index("col")
    self_index = lax.axis_index("row") * tm_count + lax.axis_index("tm")
    row_series = lax.all_gather(whitened, "col", axis=1, tiled=True)
    piece = lax.dynamic_slice_in_dim(row_series, slab_offset + col_index * PANEL, PANEL, 1)
    slab_part = broadcast(piece, ("row", "tm"), owner_index)
    covariance = (
        lax.dot_general(
            row_series, slab_part, (((0,), (0,)), ((), ())), preferred_element_type=jnp.float32
        )
        * scale
    )
    owner_flag = (self_index == owner_index).astype(jnp.float32)
    ridge_rows = slab_offset + col_index * PANEL
    zero_index = jnp.zeros((), jnp.int32)
    diag_block = (
        lax.dynamic_slice(covariance, (ridge_rows, zero_index), (PANEL, PANEL))
        + jnp.diag(ridge) * owner_flag
    )
    covariance = lax.dynamic_update_slice(covariance, diag_block, (ridge_rows, zero_index))
    identity = jnp.eye(PANEL, dtype=jnp.float32)
    factors = []
    finished = col_index < 0
    for section in range(PANELS):
        panel_index = panels[section]
        finished = finished | (col_index == panel_index)
        pivot_local = lax.dynamic_slice_in_dim(
            covariance, slab_offset + panel_index * PANEL, PANEL, 0
        )
        pivot_rows = from_root(pivot_local, ("row", "tm"), owner_index)
        pivot_safe = jnp.where(col_index == panel_index, pivot_rows, identity)
        lower_factor = jnp.linalg.cholesky(pivot_safe)
        panel_now = jax.scipy.linalg.solve_triangular(lower_factor, covariance.T, lower=True).T
        small_block = lower_factor
        panel_bf = broadcast_2(panel_now.astype(jnp.bfloat16), "col", panel_index)
        small_block = broadcast_2(small_block, "col", panel_index)
        coupling = jax.scipy.linalg.solve_triangular(small_block, pivot_rows, lower=True).T
        coupling_bf = coupling.astype(jnp.bfloat16)
        covariance = covariance - lax.dot_general(
            panel_bf, coupling_bf, (((1,), (1,)), ((), ())), preferred_element_type=jnp.float32
        )
        factors.append(panel_bf)
    trailing = jnp.where(finished, jnp.zeros_like(covariance), covariance)
    return (trailing, jnp.stack(factors))


def solution(mesh):
    in_specs = (P("row", None, "tm", "col"), P(), P("col"), P(), P())
    out_specs = (P(("row", "tm"), "col"), P(None, ("row", "tm"), None))
    return jax.shard_map(
        on_device, mesh=mesh, in_specs=in_specs, out_specs=out_specs, check_vma=False
    )
```

profile of v0, /device:TPU:1, one launch (start us, length us, event | category | flops | bytes accessed | tf_op | source)
XLA Modules:
  0.0 1696.4 jit_solution(11098721160999571711)
XLA Ops:
  10.1 34.7 %all_to_all.15 = bf16[64,16,1,1024]{3,0,2,1:T(8,128)(2,1)S(1)} all-to-all(bf16[64,16,1,1024]{3,0,2,1:T(8,128)(2,1)S(1)} %copy.24), channel_id=1, replica_groups=mesh['row'=16,'col'=4,'tm'=2] {'row'}, dimensions={1} | all-to-all | bytes 4194304 | tf_op jit(solution)/shard_map/all_to_all | solution.py:37
  49.3 62.6 %all-gather.12.cloned.1.call-done = bf16[1024,4096]{1,0:T(8,128)(2,1)} async-done(((bf16[1024,1024]{1,0:T(8,128)(2,1)}), bf16[1024,4096]{1,0:T(8,128)(2,1)}) %all-gather.12.cloned.1.call-update) | async-done | bytes 8388624 | tf_op jit(solution)/shard_map/all_gather | solution.py:51
  116.0 284.7 %all-reduce.3.cloned.1.call-done = bf16[1024,512]{1,0:T(8,128)(2,1)} async-done(((bf16[1024,512]{1,0:T(8,128)(2,1)}), bf16[1024,512]{1,0:T(8,128)(2,1)}) %all-reduce.3.cloned.1.call-update) | async-done | bytes 1048592 | tf_op jit(solution)/shard_map/psum | solution.py:13
  420.8 160.0 %reduce-scatter.7.cloned.1.call-done = f32[16,512]{1,0:T(8,128)} async-done(((f32[512,512]{1,0:T(8,128)}), f32[16,512]{1,0:T(8,128)}) %reduce-scatter.7.cloned.1.call-update) | async-done | bytes 32784 | tf_op jit(solution)/shard_map/reduce_scatter | solution.py:28
  581.7 149.1 %all-gather.14.cloned.1.call-done = f32[512,512]{1,0:T(8,128)} async-done(((f32[16,512]{1,0:T(8,128)}), f32[512,512]{1,0:T(8,128)}) %all-gather.14.cloned.1.call-update) | async-done | bytes 1048592 | tf_op jit(solution)/shard_map/all_gather | solution.py:29
  733.1 11.7 cholesky.286
  755.5 11.7 cholesky.305
  767.2 10.2 custom-call.32
  778.1 11.7 cholesky.326
  800.9 11.9 cholesky.343
  826.0 39.3 %custom-call.34 = f32[4,128,128]{1,2,0:T(8,128)S(1)} custom-call(f32[4,128,128]{2,1,0:T(8,128)S(1)} %get-tuple-element.33), custom_call_target="InvertDiagBlocksLowerTriangular" | custom-call | tf_op jit(solution)/shard_map/jit(_solve_triangular)/triangular_solve | solution.py:80
  902.4 39.3 %custom-call.35 = f32[4,128,128]{1,2,0:T(8,128)S(1)} custom-call(f32[4,128,128]{2,1,0:T(8,128)S(1)} %get-tuple-element.34), custom_call_target="InvertDiagBlocksLowerTriangular" | custom-call | tf_op jit(solution)/shard_map/jit(_solve_triangular)/triangular_solve | solution.py:84
  944.8 78.1 %all-gather.18.cloned.1.call-done = bf16[16384,512]{0,1:T(8,128)(2,1)} async-done(((bf16[4096,512]{0,1:T(8,128)(2,1)}), bf16[16384,512]{0,1:T(8,128)(2,1)}) %all-gather.18.cloned.1.call-update) | async-done | bytes 16777232 | tf_op jit(solution)/shard_map/all_gather | solution.py:33
  1022.9 22.4 %copy.40 = bf16[16384,512]{1,0:T(8,128)(2,1)} copy(bf16[16384,512]{0,1:T(8,128)(2,1)} %all-gather.18.cloned.1.call-done) | data formatting | bytes 33554432 | tf_op jit(solution)/shard_map/all_gather | solution.py:33
  1060.6 136.3 %reduce-scatter.9.cloned.1.call-done = f32[16,512]{1,0:T(8,128)} async-done(((f32[512,512]{1,0:T(8,128)}), f32[16,512]{1,0:T(8,128)}) %reduce-scatter.9.cloned.1.call-update) | async-done | bytes 32784 | tf_op jit(solution)/shard_map/reduce_scatter | solution.py:28
  1197.7 149.6 %all-gather.16.cloned.1.call-done = f32[512,512]{1,0:T(8,128)} async-done(((f32[16,512]{1,0:T(8,128)}), f32[512,512]{1,0:T(8,128)}) %all-gather.16.cloned.1.call-update) | async-done | bytes 1048592 | tf_op jit(solution)/shard_map/all_gather | solution.py:29
  1349.6 11.7 cholesky.358
  1372.6 11.7 cholesky.377
  1395.9 11.7 cholesky.398
  1418.8 11.9 cholesky.415
  1442.8 39.3 %custom-call.39 = f32[4,128,128]{1,2,0:T(8,128)S(1)} custom-call(f32[4,128,128]{2,1,0:T(8,128)S(1)} %get-tuple-element.35), custom_call_target="InvertDiagBlocksLowerTriangular" | custom-call | tf_op jit(solution)/shard_map/jit(_solve_triangular)/triangular_solve | solution.py:80
  1518.8 39.3 %custom-call.40 = f32[4,128,128]{1,2,0:T(8,128)S(1)} custom-call(f32[4,128,128]{2,1,0:T(8,128)S(1)} %get-tuple-element.36), custom_call_target="InvertDiagBlocksLowerTriangular" | custom-call | tf_op jit(solution)/shard_map/jit(_solve_triangular)/triangular_solve | solution.py:84
  1561.3 78.4 %all-gather.22.cloned.1.call-done = bf16[16384,512]{0,1:T(8,128)(2,1)} async-done(((bf16[4096,512]{0,1:T(8,128)(2,1)}), bf16[16384,512]{0,1:T(8,128)(2,1)}) %all-gather.22.cloned.1.call-update) | async-done | bytes 16777232 | tf_op jit(solution)/shard_map/all_gather | solution.py:33
  1639.7 22.6 %copy.41 = bf16[16384,512]{1,0:T(8,128)(2,1)} copy(bf16[16384,512]{0,1:T(8,128)(2,1)} %all-gather.22.cloned.1.call-done) | data formatting | bytes 33554432 | tf_op jit(solution)/shard_map/all_gather | solution.py:33
  (197 shorter events, 261.0 us)
Async XLA Ops:
  7.2 37.7 %copy-start = (bf16[1024,1024]{1,0:T(8,128)(2,1)S(1)}, bf16[1024,1024]{1,0:T(8,128)(2,1)}, u32[]{:S(2)}) copy-start(bf16[1024,1024]{1,0:T(8,128)(2,1)} %param.11) | copy-start | bytes 6291460
  7.2 104.7 %all-gather.12.cloned.1.call-start = ((), (), s32[]{:S(2)}) async-start(), calls=%async_computation.3 | async-start | bytes 10485760 | tf_op jit(solution)/shard_map/all_gather | solution.py:51
  48.5 66.2 %copy-start.8 = (s32[4]{0:T(128)S(1)}, s32[4]{0:T(128)}, u32[]{:S(2)}) copy-start(s32[4]{0:T(128)} %param.14) | copy-start | bytes 52
  48.5 352.1 %all-reduce.3.cloned.1.call-start = ((), (), s32[]{:S(2)}) async-start(), calls=%async_computation.4 | async-start | bytes 2097152 | tf_op jit(solution)/shard_map/psum | solution.py:13
  114.7 466.1 %reduce-scatter.7.cloned.1.call-start = ((), (), s32[]{:S(2)}) async-start(), calls=%async_computation.11 | async-start | bytes 1081344 | tf_op jit(solution)/shard_map/reduce_scatter | solution.py:28
  116.0 295.6 %copy-start.7 = (f32[512]{0:T(512)S(1)}, f32[512]{0:T(512)}, u32[]{:S(2)}) copy-start(f32[512]{0:T(512)} %param.12) | copy-start | bytes 6148
  408.2 3.4 copy-start.3
  420.8 310.0 %all-gather.14.cloned.1.call-start = ((), (), s32[]{:S(2)}) async-start(), calls=%async_computation.5 | async-start | bytes 1081344 | tf_op jit(solution)/shard_map/all_gather | solution.py:29
  580.9 312.3 %all-gather.20.cloned.1.call-start = ((), (), s32[]{:S(2)}) async-start(), calls=%async_computation.8 | async-start | bytes 5242880 | tf_op jit(solution)/shard_map/all_gather | solution.py:33
  817.9 205.1 %all-gather.18.cloned.1.call-start = ((), (), s32[]{:S(2)}) async-start(), calls=%async_computation.7 | async-start | bytes 20971520 | tf_op jit(solution)/shard_map/all_gather | solution.py:33
  890.6 51.0 %copy-start.5 = (f32[512,512]{1,0:T(8,128)S(1)}, f32[512,512]{1,0:T(8,128)}, u32[]{:S(2)}) copy-start(f32[512,512]{1,0:T(8,128)} %all-gather.14.cloned.1.call-done) | copy-start | bytes 3145732
  890.7 306.2 %reduce-scatter.9.cloned.1.call-start = ((), (), s32[]{:S(2)}) async-start(), calls=%async_computation.12 | async-start | bytes 1081344 | tf_op jit(solution)/shard_map/reduce_scatter | solution.py:28
  1047.8 7.6 copy-start.4
  1055.4 3.4 copy-start.2
  1060.5 286.8 %all-gather.16.cloned.1.call-start = ((), (), s32[]{:S(2)}) async-start(), calls=%async_computation.6 | async-start | bytes 1081344 | tf_op jit(solution)/shard_map/all_gather | solution.py:29
  1196.9 312.3 %all-gather.24.cloned.1.call-start = ((), (), s32[]{:S(2)}) async-start(), calls=%async_computation.10 | async-start | bytes 5242880 | tf_op jit(solution)/shard_map/all_gather | solution.py:33
  1435.0 204.7 %all-gather.22.cloned.1.call-start = ((), (), s32[]{:S(2)}) async-start(), calls=%async_computation.9 | async-start | bytes 20971520 | tf_op jit(solution)/shard_map/all_gather | solution.py:33
  1507.1 51.0 %copy-start.6 = (f32[512,512]{1,0:T(8,128)S(1)}, f32[512,512]{1,0:T(8,128)}, u32[]{:S(2)}) copy-start(f32[512,512]{1,0:T(8,128)} %all-gather.16.cloned.1.call-done) | copy-start | bytes 3145732
  1680.2 9.1 copy-start.1
Sparse Core Ops, SparseCore 0:
  48.7 63.1 all-gather.11
  114.9 285.7 all-reduce.2
  420.9 159.9 reduce-scatter.6
  582.3 148.4 all-gather.13
  818.0 60.6 all-gather.19
  890.8 132.0 all-gather.17
  1060.6 136.1 reduce-scatter.8
  1198.6 148.7 all-gather.15
  1435.2 61.2 all-gather.23
  1507.3 132.3 all-gather.21
where the time goes:
time: 1700 us
  waiting for transfers between devices  1100 us (65%)
  other arithmetic  338 us (20%)
  local copies, waits for them, and re-layouts  113 us (7%)
  matrix products  83.3 us (5%)
  blocking collectives  34.7 us (2%)
  between operations  26.9 us (2%)
    all_gather x2, waiting for transfers between devices, from_root(): lax.all_gather(own, axis, axis=0, tiled=True)[:len(lines)]  299 us
    reduce_scatter x2, waiting for transfers between devices, from_root(): own = lax.psum_scatter(padded, axis, scatter_dimension=0, tiled=True)  296 us
    psum x1, waiting for transfers between devices, broadcast(): return lax.psum(block, axis)  285 us
    another operation x29, other arithmetic, on_device(): lower_factor = jnp.linalg.cholesky(pivot_safe)  158 us
    all_gather x4, waiting for transfers between devices, broadcast_2(): lax.all_gather(shard, axis)  157 us
    another operation x4, other arithmetic, on_device(): jax.scipy.linalg.solve_triangular(small_block, pivot_rows, lower=True)  81.3 us
    another operation x5, other arithmetic, on_device(): jax.scipy.linalg.solve_triangular(lower_factor, covariance.T, lower=True)  81.2 us
    all_gather x1, waiting for transfers between devices, on_device(): row_series = lax.all_gather(whitened, 'col', axis=1, tiled=True)  62.6 us
  transfers between devices with their start and end apart: 10, of which 8 were waited for; matrix products, arithmetic and copies ran while one was open for 15% of the time, Pallas kernels for 0%

commit v1 on v0

v1 whole, which is shorter than its diff:
```python
import jax
import jax.numpy as jnp
from jax import lax
from jax.experimental import pallas as pl
from jax.experimental.pallas import tpu as pltpu
from jax.sharding import PartitionSpec as P

S = 1024
PANEL = 512
TILE = 512
HIGH = lax.Precision.HIGHEST


def place(y, core):
    return ((y // 2) * 2 + core) * 2 + y % 2


def y_shift(k):
    return [(place(y, m), place((y + k) % 4, m)) for y in range(4) for m in range(2)]


def x_shift(k):
    return [(x * 4 + z, ((x + k) % 4) * 4 + z) for x in range(4) for z in range(4)]


def z_shift(k):
    return [(x * 4 + z, x * 4 + (z + k) % 4) for x in range(4) for z in range(4)]


def swap(value, bit):
    return lax.ppermute(value, "col", [(c, c ^ bit) for c in range(4)])


def ring_gather(piece, axis, shift, own):
    full = jnp.zeros((4,) + piece.shape, piece.dtype)
    full = lax.dynamic_update_index_in_dim(full, piece, own, 0)
    for k in range(1, 4):
        got = lax.ppermute(piece, axis, shift(k))
        full = lax.dynamic_update_index_in_dim(full, got, (own - k) % 4, 0)
    return full


def dot_t(a, b):
    return lax.dot_general(a, b, (((0,), (0,)), ((), ())), preferred_element_type=jnp.float32)


def dot_tf(a, b):
    return lax.dot_general(a, b, (((0,), (0,)), ((), ())), precision=HIGH)


def dot_nt(a, b):
    return lax.dot_general(a, b, (((1,), (1,)), ((), ())), precision=HIGH)


def split(value):
    high = value.astype(jnp.bfloat16)
    return high, (value - high.astype(jnp.float32)).astype(jnp.bfloat16)


def finish_kernel(
    info, x0, x1, x2, x3, w0h, w0l, w1h, w1l, vh, vl, sc, f0, f1, r0, r1, dc, t_ref, f_ref, x
):
    i = pl.program_id(0)
    for m, source in enumerate((x0, x1, x2, x3)):
        @pl.when(i // 2 == m)
        def _(source=source):
            x[...] = source[...]

    tile = (info[0] ^ (i // 2)) * 2 + i % 2
    xs = x[...]

    def dot(a, b):
        return jnp.dot(a, b[...], preferred_element_type=jnp.float32)

    on0 = (tile == info[1]).astype(jnp.float32)
    on1 = (tile == info[2]).astype(jnp.float32)
    p0 = (dot(xs, w0h) + dot(xs, w0l)) * (1.0 / 32.0) + on0 * r0[...]
    p0 = p0.astype(jnp.bfloat16)
    f_ref[0] = p0
    p1 = (dot(xs, w1h) + dot(xs, w1l)) * (1.0 / 32.0) - (dot(p0, vh) + dot(p0, vl)) + on1 * r1[...]
    p1 = p1.astype(jnp.bfloat16)
    f_ref[1] = p1

    @pl.when(info[4] == 1)
    def _():
        t_ref[...] = jnp.zeros_like(t_ref)

    @pl.when(info[4] == 0)
    def _():
        onc = (tile == info[3]).astype(jnp.float32)
        diagonal = lax.broadcasted_iota(jnp.int32, (TILE, PANEL), 0) == lax.broadcasted_iota(
            jnp.int32, (TILE, PANEL), 1
        )
        add = jnp.where(diagonal, onc * dc[...], 0.0)
        t_ref[...] = dot(xs, sc) * (1.0 / 32.0) + add - dot(p0, f0) - dot(p1, f1)


def finish(info, xs, consts):
    def tile(i, info):
        return (info[0] ^ (i // 2)) * 2 + i % 2

    def x_spec(m):
        return pl.BlockSpec(
            (TILE, S), lambda i, info: (jnp.where(i // 2 == m, i % 2, jnp.where(i // 2 < m, 0, 1)), 0)
        )

    def const_spec(value):
        return pl.BlockSpec(value.shape, lambda i, info: (0, 0), pipeline_mode=pl.Buffered(1))

    return pl.pallas_call(
        finish_kernel,
        out_shape=(
            jax.ShapeDtypeStruct((4 * S, PANEL), jnp.float32),
            jax.ShapeDtypeStruct((2, 4 * S, PANEL), jnp.bfloat16),
        ),
        grid_spec=pltpu.PrefetchScalarGridSpec(
            num_scalar_prefetch=1,
            grid=(8,),
            in_specs=[x_spec(m) for m in range(4)] + [const_spec(v) for v in consts],
            out_specs=(
                pl.BlockSpec((TILE, PANEL), lambda i, info: (tile(i, info), 0)),
                pl.BlockSpec((2, TILE, PANEL), lambda i, info: (0, tile(i, info), 0)),
            ),
            scratch_shapes=[pltpu.VMEM((TILE, S), jnp.bfloat16)],
        ),
        compiler_params=pltpu.CompilerParams(vmem_limit_bytes=44 << 20),
        name="finish",
    )(info, *xs, *consts)


def inverse_factor(a):
    lower = jnp.linalg.cholesky(a)
    return jax.scipy.linalg.solve_triangular(lower, jnp.eye(PANEL, dtype=jnp.float32), lower=True)


def on_device(samples, whitening, ridge, slab_start, panels):
    col = lax.axis_index("col")
    tm = lax.axis_index("tm")
    row = lax.axis_index("row")
    core = col % 2
    y = (col // 2) * 2 + tm
    slab = slab_start[0]
    half, owner_tm, owner_row = slab % 2, (slab // 2) % 2, slab // 4
    local = samples[:, :, 0, :]

    ridges = jnp.zeros((4, PANEL), jnp.float32)
    ridges = lax.dynamic_update_index_in_dim(ridges, ridge, col, 0)
    for bit in (1, 2, 3):
        ridges = lax.dynamic_update_index_in_dim(ridges, swap(ridge, bit), col ^ bit, 0)
    q0, q1 = panels[0], panels[1]
    ridge0 = lax.dynamic_index_in_dim(ridges, q0, 0, keepdims=False)
    ridge1 = lax.dynamic_index_in_dim(ridges, q1, 0, keepdims=False)

    mine = lax.dynamic_index_in_dim(local, owner_row, 1, keepdims=False)
    away = (y - (half * 2 + owner_tm)) % 4
    part = mine
    for k in range(1, 4):
        got = lax.ppermute(mine, ("col", "tm"), y_shift(k))
        part = jnp.where(away == k, got, part)
    line = ring_gather(part, "row", x_shift, row // 4)
    plane = ring_gather(line, "row", z_shift, row % 4)
    raw = plane.transpose(1, 0, 2, 3).reshape(S, S)
    half_slab = jnp.dot(whitening, raw, preferred_element_type=jnp.float32).astype(jnp.bfloat16)
    other = swap(half_slab, 1)
    slabs = jnp.zeros((2, S, S), jnp.bfloat16)
    slabs = lax.dynamic_update_index_in_dim(slabs, half_slab, core, 0)
    slabs = lax.dynamic_update_index_in_dim(slabs, other, 1 - core, 0)

    def panel_of(q):
        return lax.dynamic_slice(slabs, (q // 2, 0, (q % 2) * PANEL), (1, S, PANEL))[0]

    s0, s1, sc = panel_of(q0), panel_of(q1), panel_of(col)

    moved = lax.all_to_all(local, "row", split_axis=1, concat_axis=0, tiled=True)
    series = moved.reshape(S, S)
    own = lax.dot_general(
        series, whitening, (((0,), (1,)), ((), ())), preferred_element_type=jnp.float32
    ).astype(jnp.bfloat16)
    far = swap(own, 2)
    xs = (own, swap(own, 1), far, swap(far, 1))

    scale = 1.0 / 32.0
    a = dot_t(s0, s0) * scale + jnp.diag(ridge0)
    b = dot_t(s0, s1) * scale
    d = dot_t(s1, s1) * scale + jnp.diag(ridge1)
    e0 = dot_t(s0, sc) * scale
    e1 = dot_t(s1, sc) * scale
    inv0 = inverse_factor(a)
    u = jnp.dot(inv0, b, precision=HIGH).astype(jnp.bfloat16)
    f0 = jnp.dot(inv0, e0, precision=HIGH).astype(jnp.bfloat16)
    inv1 = inverse_factor(d - dot_t(u, u))
    f1 = jnp.dot(inv1, e1 - dot_t(u, f0), precision=HIGH).astype(jnp.bfloat16)
    w0 = split(dot_nt(s0.astype(jnp.float32), inv0))
    w1 = split(dot_nt(s1.astype(jnp.float32), inv1))
    v = split(dot_nt(u.astype(jnp.float32), inv1))
    r0 = ridge0[:, None] * inv0.T
    r1 = ridge1[:, None] * inv1.T

    holds = (row == owner_row) & (tm == owner_tm)
    first = half * 4
    done = (col == q0) | (col == q1)

    def slab_tile(q):
        return jnp.where(holds, first + q, -1)

    info = jnp.stack([col, slab_tile(q0), slab_tile(q1), slab_tile(col), done.astype(jnp.int32)])
    consts = (*w0, *w1, *v, sc, f0, f1, r0, r1, ridge[None, :])
    return finish(info.astype(jnp.int32), xs, consts)


def solution(mesh):
    in_specs = (P("row", None, "tm", "col"), P(), P("col"), P(), P())
    out_specs = (P(("row", "tm"), "col"), P(None, ("row", "tm"), None))
    return jax.shard_map(
        on_device, mesh=mesh, in_specs=in_specs, out_specs=out_specs, check_vma=False
    )
```

time: 1700 us -> 511 us (0.30)
  waiting for transfers between devices: 1100 us -> 39.5 us
  other arithmetic: 338 us -> 254 us
  local copies, waits for them, and re-layouts: 113 us -> 51.5 us
  Pallas kernels: 0 us -> 40.2 us
  blocking collectives: 34.7 us -> 0 us
  starting transfers between devices: 0.76 us -> 30.5 us
    all_gather x7 -> x0, waiting for transfers between devices: 518 us -> none  [the longest x2 299 us: from_root(): lax.all_gather(own, axis, axis=0, tiled=True)[:len(lines)]]
    reduce_scatter x2 -> x0, waiting for transfers between devices: 296 us -> none  [from_root(): own = lax.psum_scatter(padded, axis, scatter_dimension=0, tiled=True)]
    psum x1 -> x0, waiting for transfers between devices: 285 us -> none  [broadcast(): return lax.psum(block, axis)]
    another operation x39 -> x34, other arithmetic: 327 us -> 252 us  [the longest x29 172 us: inverse_factor(): lower = jnp.linalg.cholesky(a)]
    all_gather x4 -> x0, local copies, waits for them, and re-layouts: 48.1 us -> none  [the longest x2 45 us: broadcast_2(): lax.all_gather(shard, axis)]
    pallas_call x0 -> x1, Pallas kernels: none -> 40.2 us  [finish(): pl.pallas_call(finish_kernel, out_shape=(jax.ShapeDtypeStruct((4 * S, PAN...]
    ppermute x0 -> x16, waiting for transfers between devices: none -> 39.5 us  [the longest x6 34.8 us: ring_gather(): got = lax.ppermute(piece, axis, shift(k))]
    all_to_all x1 -> x0, blocking collectives: 34.7 us -> none  [on_device(): lax.all_to_all(samples, 'row', split_axis=1, concat_axis=0, tiled=True)]
  transfers between devices with their start and end apart: 10 -> 17, of which waited for: 8 -> 7; matrix products, arithmetic and copies ran while one was open for 15% -> 74% of each run, Pallas kernels for 0% -> 0%
where the time goes in v1:
time: 511 us; the launch traced here: 506 us
  other arithmetic  254 us (50%)
  matrix products  72.1 us (14%)
  local copies, waits for them, and re-layouts  51.5 us (10%)
  Pallas kernels  40.2 us (8%)
  waiting for transfers between devices  39.5 us (8%)
  starting transfers between devices  30.5 us (6%)
  between operations  18.1 us (4%)
    another operation x29, other arithmetic, inverse_factor(): lower = jnp.linalg.cholesky(a)  172 us
    another operation x5, other arithmetic, inverse_factor(): jax.scipy.linalg.solve_triangular(lower, jnp.eye(PANEL, dtype=jnp.float32...  80 us
    pallas_call x1, Pallas kernels, finish(): pl.pallas_call(finish_kernel, out_shape=(jax.ShapeDtypeStruct((4 * S, PAN...  40.2 us
    ppermute x6, waiting for transfers between devices, ring_gather(): got = lax.ppermute(piece, axis, shift(k))  34.8 us
    another operation x33, local copies, waits for them, and re-layouts, inverse_factor(): jax.scipy.linalg.solve_triangular(lower, jnp.eye(PANEL, dtype=jnp.float32...  23.8 us
    another operation x14, matrix products, inverse_factor(): jax.scipy.linalg.solve_triangular(lower, jnp.eye(PANEL, dtype=jnp.float32...  18.3 us
    another operation x12, matrix products, inverse_factor(): lower = jnp.linalg.cholesky(a)  12.7 us
    dot_general x7, matrix products, dot_t(): lax.dot_general(a, b, (((0,), (0,)), ((), ())), preferred_element_type=jn...  12.4 us
  transfers between devices with their start and end apart: 17, of which 7 were waited for; matrix products, arithmetic and copies ran while one was open for 74% of the time, Pallas kernels for 0%

profile of v1, /device:TPU:1, one launch (start us, length us, event | category | flops | bytes accessed | tf_op | source)
XLA Modules:
  0.0 505.7 jit_solution(8094995665116199095)
XLA Ops:
  27.6 4.1 copy.52
  31.6 4.4 all-to-all-start
  39.9 27.3 %collective-permute-done.10 = bf16[4,64,1024]{2,1,0:T(8,128)(2,1)S(1)} collective-permute-done((bf16[4,64,1024]{2,1,0:T(8,128)(2,1)S(1)}, bf16[4,64,1024]{2,1,0:T(8,128)(2,1)S(1)}, u32[]{:S(2)}, u32[]{:S(2)}) %collective-permute-start.10) | collective-permute-done | bytes 524320 | tf_op jit(solution)/shard_map/ppermute | solution.py:38
  100.4 5.3 %convolution_convert_fusion.1.x0 = bf16[1024,1024]{1,0:T(8,128)(2,1)} fusion(bf16[1024,1024]{1,0:T(8,128)(2,1)} %bitcast.11, bf16[1024,1024]{1,0:T(8,128)(2,1)S(1)} %copy-done), kind=kOutput, calls=%fused_computation.8 | convolution fusion | flops 2148532224 | bytes 6291456 | tf_op jit(solution)/shard_map/dot_general | solution.py:176
  115.9 11.7 %cholesky.286 = f32[128,128]{1,0:T(8,128)S(1)} custom-call(f32[128,128]{1,0:T(8,128)S(1)} %cholesky.426), custom_call_target="Cholesky" | custom-call | tf_op jit(solution)/shard_map/jit(cholesky)/cholesky | solution.py:132
  127.7 9.8 %custom-call.27 = f32[1,128,128]{1,2,0:T(8,128)S(1)} custom-call(f32[1,128,128]{2,1,0:T(8,128)S(1)} %get-tuple-element.67), custom_call_target="InvertDiagBlocksLowerTriangular" | custom-call | tf_op jit(solution)/shard_map/jit(cholesky)/cholesky | solution.py:132
  140.1 11.7 %cholesky.305 = f32[128,128]{1,0:T(8,128)S(1)} custom-call(f32[128,128]{1,0:T(8,128)S(1)} %cholesky.430), custom_call_target="Cholesky" | custom-call | tf_op jit(solution)/shard_map/jit(cholesky)/cholesky | solution.py:132
  151.9 18.5 %custom-call.28 = f32[1,128,128]{1,2,0:T(8,128)S(1)} custom-call(f32[1,128,128]{2,1,0:T(8,128)S(1)} %get-tuple-element.64), custom_call_target="InvertDiagBlocksLowerTriangular" | custom-call | tf_op jit(solution)/shard_map/jit(cholesky)/cholesky | solution.py:132
  171.9 11.7 %cholesky.326 = f32[128,128]{1,0:T(8,128)S(1)} custom-call(f32[128,128]{1,0:T(8,128)S(1)} %cholesky.435), custom_call_target="Cholesky" | custom-call | tf_op jit(solution)/shard_map/jit(cholesky)/cholesky | solution.py:132
  184.3 9.8 %custom-call.29 = f32[1,128,128]{1,2,0:T(8,128)S(1)} custom-call(f32[1,128,128]{2,1,0:T(8,128)S(1)} %get-tuple-element.61), custom_call_target="InvertDiagBlocksLowerTriangular" | custom-call | tf_op jit(solution)/shard_map/jit(cholesky)/cholesky | solution.py:132
  195.6 12.1 %cholesky.343 = f32[128,128]{1,0:T(8,128)S(1)} custom-call(f32[128,128]{1,0:T(8,128)S(1)} %convolution_subtract_fusion.13), custom_call_target="Cholesky" | custom-call | tf_op jit(solution)/shard_map/jit(cholesky)/cholesky | solution.py:132
  211.8 7.7 %while.4 = (s32[]{:T(128)}, f32[512,512]{1,0:T(8,128)S(1)}, s32[4,2]{0,1:T(2,128)S(1)}, f32[4,128,128]{2,1,0:T(8,128)S(1)}, s32[]{:T(128)}) while((s32[]{:T(128)}, f32[512,512]{1,0:T(8,128)S(1)}, s32[4,2]{0,1:T(2,128)S(1)}, f32[4,128,128]{2,1,0:T(8,128)S(1)}, s32[]{:T(128)}) %tuple.59), condition=%wide.while_cond, body=%wide.while_body.sunk | while | flops 2 | bytes 131189 | solution.py:133
  219.5 39.3 %custom-call.30 = f32[4,128,128]{1,2,0:T(8,128)S(1)} custom-call(f32[4,128,128]{2,1,0:T(8,128)S(1)} %get-tuple-element.18), custom_call_target="InvertDiagBlocksLowerTriangular" | custom-call | tf_op jit(solution)/shard_map/jit(_solve_triangular)/triangular_solve | solution.py:133
  280.9 11.9 %cholesky.358 = f32[128,128]{1,0:T(8,128)S(1)} custom-call(f32[128,128]{1,0:T(8,128)S(1)} %cholesky.439), custom_call_target="Cholesky" | custom-call | tf_op jit(solution)/shard_map/jit(cholesky)/cholesky | solution.py:132
  293.5 9.8 %custom-call.31 = f32[1,128,128]{1,2,0:T(8,128)S(1)} custom-call(f32[1,128,128]{2,1,0:T(8,128)S(1)} %get-tuple-element.57), custom_call_target="InvertDiagBlocksLowerTriangular" | custom-call | tf_op jit(solution)/shard_map/jit(cholesky)/cholesky | solution.py:132
  306.7 11.7 %cholesky.377 = f32[128,128]{1,0:T(8,128)S(1)} custom-call(f32[128,128]{1,0:T(8,128)S(1)} %cholesky.443), custom_call_target="Cholesky" | custom-call | tf_op jit(solution)/shard_map/jit(cholesky)/cholesky | solution.py:132
  319.1 9.8 %custom-call.32 = f32[1,128,128]{1,2,0:T(8,128)S(1)} custom-call(f32[1,128,128]{2,1,0:T(8,128)S(1)} %get-tuple-element.54), custom_call_target="InvertDiagBlocksLowerTriangular" | custom-call | tf_op jit(solution)/shard_map/jit(cholesky)/cholesky | solution.py:132
  332.0 13.6 %cholesky.398 = f32[128,128]{1,0:T(8,128)} custom-call(f32[128,128]{1,0:T(8,128)} %cholesky.448), custom_call_target="Cholesky" | custom-call | tf_op jit(solution)/shard_map/jit(cholesky)/cholesky | solution.py:132
  347.8 11.3 %custom-call.33 = f32[1,128,128]{1,2,0:T(8,128)} custom-call(f32[1,128,128]{2,1,0:T(8,128)} %get-tuple-element.51), custom_call_target="InvertDiagBlocksLowerTriangular" | custom-call | tf_op jit(solution)/shard_map/jit(cholesky)/cholesky | solution.py:132
  361.3 11.7 %cholesky.415 = f32[128,128]{1,0:T(8,128)S(1)} custom-call(f32[128,128]{1,0:T(8,128)S(1)} %convolution_subtract_fusion.12), custom_call_target="Cholesky" | custom-call | tf_op jit(solution)/shard_map/jit(cholesky)/cholesky | solution.py:132
  377.5 12.0 %while.5 = (s32[]{:T(128)}, f32[512,512]{1,0:T(8,128)}, s32[4,2]{0,1:T(2,128)S(1)}, f32[4,128,128]{2,1,0:T(8,128)S(1)}, s32[]{:T(128)}) while((s32[]{:T(128)}, f32[512,512]{1,0:T(8,128)}, s32[4,2]{0,1:T(2,128)S(1)}, f32[4,128,128]{2,1,0:T(8,128)S(1)}, s32[]{:T(128)}) %tuple.65), condition=%wide.while_cond.clone, body=%wide.while_body.clone.sunk | while | flops 2 | bytes 131189 | solution.py:133
  389.5 39.5 %custom-call.34 = f32[4,128,128]{1,2,0:T(8,128)S(1)} custom-call(f32[4,128,128]{2,1,0:T(8,128)S(1)} %get-tuple-element.19), custom_call_target="InvertDiagBlocksLowerTriangular" | custom-call | tf_op jit(solution)/shard_map/jit(_solve_triangular)/triangular_solve | solution.py:133
  429.0 4.6 subtract_convert_fusion.1
  465.3 40.2 %finish.1 = (f32[4096,512]{1,0:T(8,128)}, bf16[2,4096,512]{2,1,0:T(8,128)(2,1)}) custom-call(s32[5]{0:T(128)S(1)} %stack.27.info, bf16[1024,1024]{1,0:T(8,128)(2,1)} %convolution_convert_fusion.1.x0, bf16[1024,1024]{1,0:T(8,128)(2,1)} %collective-permute-done.x1, bf16[1024,1024]{1,0:T(8,128)(2,1)} %collective-permute-done.1.x2, ...), custom_call_target="tpu_custom_call" | custom-call | tf_op jit(solution)/shard_map/finish/pallas_call | solution.py:110
  (225 shorter events, 157.7 us)
Async XLA Ops:
  0.6 70.3 %copy-start = (bf16[1024,1024]{1,0:T(8,128)(2,1)S(1)}, bf16[1024,1024]{1,0:T(8,128)(2,1)}, u32[]{:S(2)}) copy-start(bf16[1024,1024]{1,0:T(8,128)(2,1)} %param.9) | copy-start | bytes 6291460
  3.0 6.7 %collective-permute-start.5 = (bf16[64,1024]{1,0:T(8,128)(2,1)S(1)}, bf16[64,1024]{1,0:T(8,128)(2,1)S(1)}, u32[]{:S(2)}, u32[]{:S(2)}) collective-permute-start(bf16[64,1024]{1,0:T(8,128)(2,1)S(1)} %bitcast.202), channel_id=1, source_target_pairs={{0,1},{2,3},{1,4},{3,6},{4,5},{6,7},{5,0},{7,2},{8,9},{10,11},{9,1... | collective-permute-start | bytes 393224 | tf_op jit(solution)/shard_map/ppermute | solution.py:158
  5.2 8.3 %collective-permute-start.4 = (bf16[64,1024]{1,0:T(8,128)(2,1)S(1)}, bf16[64,1024]{1,0:T(8,128)(2,1)S(1)}, u32[]{:S(2)}, u32[]{:S(2)}) collective-permute-start(bf16[64,1024]{1,0:T(8,128)(2,1)S(1)} %bitcast.203), channel_id=1, source_target_pairs={{0,4},{2,6},{1,5},{3,7},{4,0},{6,2},{5,1},{7,3},{8,12},{10,14},{9,... | collective-permute-start | bytes 393224 | tf_op jit(solution)/shard_map/ppermute | solution.py:158
  7.8 5.7 %collective-permute-start.3 = (bf16[64,1024]{1,0:T(8,128)(2,1)S(1)}, bf16[64,1024]{1,0:T(8,128)(2,1)S(1)}, u32[]{:S(2)}, u32[]{:S(2)}) collective-permute-start(bf16[64,1024]{1,0:T(8,128)(2,1)S(1)} %bitcast.204), channel_id=1, source_target_pairs={{0,5},{2,7},{1,0},{3,2},{4,1},{6,3},{5,4},{7,6},{8,13},{10,15},{9,... | collective-permute-start | bytes 393224 | tf_op jit(solution)/shard_map/ppermute | solution.py:158
  13.7 5.1 %collective-permute-start.6 = (bf16[64,1024]{1,0:T(8,128)(2,1)S(1)}, bf16[64,1024]{1,0:T(8,128)(2,1)S(1)}, u32[]{:S(2)}, u32[]{:S(2)}) collective-permute-start(bf16[64,1024]{1,0:T(8,128)(2,1)S(1)} %get-tuple-element.43), channel_id=1, source_target_pairs={{0,32},{8,40},{16,48},{24,56},{32,64},{40,72},{48,80},{56,88},{64,... | collective-permute-start | bytes 393224 | tf_op jit(solution)/shard_map/ppermute | solution.py:38
  15.0 6.9 %collective-permute-start.7 = (bf16[64,1024]{1,0:T(8,128)(2,1)S(1)}, bf16[64,1024]{1,0:T(8,128)(2,1)S(1)}, u32[]{:S(2)}, u32[]{:S(2)}) collective-permute-start(bf16[64,1024]{1,0:T(8,128)(2,1)S(1)} %get-tuple-element.43), channel_id=1, source_target_pairs={{0,64},{8,72},{16,80},{24,88},{32,96},{40,104},{48,112},{56,120},{... | collective-permute-start | bytes 393224 | tf_op jit(solution)/shard_map/ppermute | solution.py:38
  17.5 5.1 %collective-permute-start.8 = (bf16[64,1024]{1,0:T(8,128)(2,1)S(1)}, bf16[64,1024]{1,0:T(8,128)(2,1)S(1)}, u32[]{:S(2)}, u32[]{:S(2)}) collective-permute-start(bf16[64,1024]{1,0:T(8,128)(2,1)S(1)} %get-tuple-element.43), channel_id=1, source_target_pairs={{0,96},{8,104},{16,112},{24,120},{32,0},{40,8},{48,16},{56,24},{64... | collective-permute-start | bytes 393224 | tf_op jit(solution)/shard_map/ppermute | solution.py:38
  22.5 16.3 %collective-permute-start.9 = (bf16[4,64,1024]{2,1,0:T(8,128)(2,1)S(1)}, bf16[4,64,1024]{2,1,0:T(8,128)(2,1)}, u32[]{:S(2)}, u32[]{:S(2)}) collective-permute-start(bf16[4,64,1024]{2,1,0:T(8,128)(2,1)S(1)} %bitcast_dynamic-update-slice_fusion.6), channel_id=1, source_target_pairs={{0,8},{8,16},{16,24},{24,0},{32,40},{40,48},{48,56},{56,32},{64,72... | collective-permute-start | bytes 1572872 | tf_op jit(solution)/shard_map/ppermute | solution.py:38
  24.3 42.9 %collective-permute-start.10 = (bf16[4,64,1024]{2,1,0:T(8,128)(2,1)S(1)}, bf16[4,64,1024]{2,1,0:T(8,128)(2,1)S(1)}, u32[]{:S(2)}, u32[]{:S(2)}) collective-permute-start(bf16[4,64,1024]{2,1,0:T(8,128)(2,1)S(1)} %bitcast_dynamic-update-slice_fusion.6), channel_id=1, source_target_pairs={{0,16},{8,24},{16,0},{24,8},{32,48},{40,56},{48,32},{56,40},{64,80... | collective-permute-start | bytes 1572872 | tf_op jit(solution)/shard_map/ppermute | solution.py:38
  31.6 68.8 %all-to-all-start = ((bf16[64,16,1024]{2,0,1:T(8,128)(2,1)}), bf16[64,16,1024]{2,0,1:T(8,128)(2,1)}, u32[]{:S(2)}, u32[]{:S(2)}) async-start(bf16[64,16,1024]{2,0,1:T(8,128)(2,1)} %bitcast.200), calls=%async_computation | async-start | bytes 4194304 | tf_op jit(solution)/shard_map/all_to_all | solution.py:174
  36.1 34.7 %collective-permute-start.11 = (bf16[4,64,1024]{2,1,0:T(8,128)(2,1)S(1)}, bf16[4,64,1024]{2,1,0:T(8,128)(2,1)S(1)}, u32[]{:S(2)}, u32[]{:S(2)}) collective-permute-start(bf16[4,64,1024]{2,1,0:T(8,128)(2,1)S(1)} %bitcast_dynamic-update-slice_fusion.6), channel_id=1, source_target_pairs={{0,24},{8,0},{16,8},{24,16},{32,56},{40,32},{48,40},{56,48},{64,88... | collective-permute-start | bytes 1572872 | tf_op jit(solution)/shard_map/ppermute | solution.py:38
  70.9 9.9 %copy-start.30 = (s32[4]{0:T(128)S(1)}, s32[4]{0:T(128)}, u32[]{:S(2)}) copy-start(s32[4]{0:T(128)} %param.12) | copy-start | bytes 52
  74.7 32.7 %collective-permute-start.12 = (bf16[1024,1024]{0,1:T(8,128)(2,1)}, bf16[1024,1024]{0,1:T(8,128)(2,1)}, u32[]{:S(2)}, u32[]{:S(2)}) collective-permute-start(bf16[1024,1024]{0,1:T(8,128)(2,1)} %bitcast.26), channel_id=1, source_target_pairs={{0,2},{2,0},{4,6},{6,4},{1,3},{3,1},{5,7},{7,5},{8,10},{10,8},{12,... | collective-permute-start | bytes 6291464 | tf_op jit(solution)/shard_map/ppermute | solution.py:31
  77.5 14.5 %collective-permute-start.13 = (f32[512]{0:T(512)S(1)}, f32[512]{0:T(512)S(1)}, u32[]{:S(2)}, u32[]{:S(2)}) collective-permute-start(f32[512]{0:T(512)S(1)} %copy-done.6), channel_id=1, source_target_pairs={{0,2},{2,0},{4,6},{6,4},{1,3},{3,1},{5,7},{7,5},{8,10},{10,8},{12,... | collective-permute-start | bytes 6152 | tf_op jit(solution)/shard_map/ppermute | solution.py:31
  77.5 14.6 %collective-permute-start.15 = (f32[512]{0:T(512)S(1)}, f32[512]{0:T(512)S(1)}, u32[]{:S(2)}, u32[]{:S(2)}) collective-permute-start(f32[512]{0:T(512)S(1)} %copy-done.6), channel_id=1, source_target_pairs={{0,6},{2,4},{4,2},{6,0},{1,7},{3,5},{5,3},{7,1},{8,14},{10,12},{12... | collective-permute-start | bytes 6152 | tf_op jit(solution)/shard_map/ppermute | solution.py:31
  79.1 12.9 %collective-permute-start.14 = (f32[512]{0:T(512)S(1)}, f32[512]{0:T(512)S(1)}, u32[]{:S(2)}, u32[]{:S(2)}) collective-permute-start(f32[512]{0:T(512)S(1)} %copy-done.6), channel_id=1, source_target_pairs={{0,4},{2,6},{4,0},{6,2},{1,5},{3,7},{5,1},{7,3},{8,12},{10,14},{12... | collective-permute-start | bytes 6152 | tf_op jit(solution)/shard_map/ppermute | solution.py:31
  92.4 19.4 %copy-start.28 = (f32[1,512]{1,0:T(1,128)}, f32[1,512]{1,0:T(1,128)S(1)}, u32[]{:S(2)}) copy-start(f32[1,512]{1,0:T(1,128)S(1)} %get-tuple-element.69) | copy-start | bytes 6148
  105.7 337.4 %collective-permute-start.1 = (bf16[1024,1024]{1,0:T(8,128)(2,1)}, bf16[1024,1024]{1,0:T(8,128)(2,1)}, u32[]{:S(2)}, u32[]{:S(2)}) collective-permute-start(bf16[1024,1024]{1,0:T(8,128)(2,1)} %convolution_convert_fusion.1.x0), channel_id=1, source_target_pairs={{0,4},{2,6},{4,0},{6,2},{1,5},{3,7},{5,1},{7,3},{8,12},{10,14},{12... | collective-permute-start | bytes 6291464 | tf_op jit(solution)/shard_map/ppermute | solution.py:31
  106.9 358.4 %collective-permute-start = (bf16[1024,1024]{1,0:T(8,128)(2,1)}, bf16[1024,1024]{1,0:T(8,128)(2,1)}, u32[]{:S(2)}, u32[]{:S(2)}) collective-permute-start(bf16[1024,1024]{1,0:T(8,128)(2,1)} %convolution_convert_fusion.1.x0), channel_id=1, source_target_pairs={{0,2},{2,0},{4,6},{6,4},{1,3},{3,1},{5,7},{7,5},{8,10},{10,8},{12,... | collective-permute-start | bytes 6291464 | tf_op jit(solution)/shard_map/ppermute | solution.py:31
  219.5 39.3 %copy-start.15 = (f32[512,512]{1,0:T(8,128)}, f32[512,512]{1,0:T(8,128)S(1)}, u32[]{:S(2)}) copy-start(f32[512,512]{1,0:T(8,128)S(1)} %get-tuple-element.172) | copy-start | bytes 3145732
  267.1 161.9 %copy-start.8 = (f32[128,512]{0,1:T(8,128)}, f32[128,512]{0,1:T(8,128)S(1)}, u32[]{:S(2)}) copy-start(f32[128,512]{0,1:T(8,128)S(1)} %copy.33) | copy-start | bytes 786436
  443.1 22.2 %collective-permute-start.2 = (bf16[1024,1024]{1,0:T(8,128)(2,1)}, bf16[1024,1024]{1,0:T(8,128)(2,1)}, u32[]{:S(2)}, u32[]{:S(2)}) collective-permute-start(bf16[1024,1024]{1,0:T(8,128)(2,1)} %collective-permute-done.1.x2), channel_id=1, source_target_pairs={{0,2},{2,0},{4,6},{6,4},{1,3},{3,1},{5,7},{7,5},{8,10},{10,8},{12,... | collective-permute-start | bytes 6291464 | tf_op jit(solution)/shard_map/ppermute | solution.py:31
  444.5 14.2 %copy-start.2 = (bf16[1024,512]{1,0:T(8,128)(2,1)}, bf16[1024,512]{1,0:T(8,128)(2,1)S(1)}, u32[]{:S(2)}) copy-start(bf16[1024,512]{1,0:T(8,128)(2,1)S(1)} %dynamic-slice_bitcast_fusion.sc) | copy-start | bytes 3145732
  465.3 40.2 %copy-start.1 = (bf16[1024,1024]{1,0:T(8,128)(2,1)S(1)}, bf16[1024,1024]{1,0:T(8,128)(2,1)}, u32[]{:S(2)}) copy-start(bf16[1024,1024]{1,0:T(8,128)(2,1)} %param.9) | copy-start | bytes 6291460
  (24 other events, 93.1 us)
